TPU v7x, 32 devices: a whole 2x2x4 slice. The times are simulated.
32 devices in a mesh: gx: 8 (over y, x, core), gy: 4 (over z).
Axes of the slice: x: 2, y: 2, z: 4, core: 2. Of those that a mesh axis runs over, the one named last changes fastest.
Arguments:
- thinker_normed: bfloat16 [4, 16, 8192], P(None, None, 'gx'), may hold values from -6 to 6
- thinker_resid: bfloat16 [4, 16, 8192], P('gy', None, 'gx'), may hold values from -6 to 6
- gate_weight: bfloat16 [8192, 29568], P('gx', 'gy'), may hold values from -0.0625 to 0.0625
- up_weight: bfloat16 [8192, 29568], P('gx', 'gy'), may hold values from -0.0625 to 0.0625
- down_weight: bfloat16 [29568, 8192], P('gy', 'gx'), may hold values from -0.03125 to 0.03125
- bridge_weight: bfloat16 [8192, 3584], P('gx'), may hold values from -0.0625 to 0.0625
- talker_stream: bfloat16 [4, 1536, 3584], P('gy', 'gx'), may hold values from -6 to 6
- norm_gain: float32 [3584], replicated, may hold values from 0.5 to 2
- w_query: bfloat16 [3584, 1792], P(None, 'gy'), may hold values from -0.09375 to 0.09375
- w_key: bfloat16 [3584, 256], P(None, 'gy'), may hold values from -0.09375 to 0.09375
- w_value: bfloat16 [3584, 256], P(None, 'gy'), may hold values from -0.09375 to 0.09375
- a_query: bfloat16 [3584, 64], replicated, may hold values from -0.09375 to 0.09375
- b_query: bfloat16 [64, 1792], replicated, may hold values from -0.75 to 0.75
- a_value: bfloat16 [3584, 64], replicated, may hold values from -0.09375 to 0.09375
- b_value: bfloat16 [64, 256], replicated, may hold values from -0.75 to 0.75
- text_index: int32 [4, 1536], P('gy', 'gx'), may hold values from 0 to 15
- span_offset: int32 [4], P('gy'), may hold values from 1 to 1535
- out_grad: bfloat16 [4, 1536, 1792], P('gy', 'gx'), may hold values from -6 to 6
Outputs:
- attn_out: bfloat16 [4, 1536, 1792], P('gy', 'gx')
- grad_aq: float32 [3584, 64], replicated
- grad_bq: float32 [64, 1792], replicated
- grad_av: float32 [3584, 64], replicated
- grad_bv: float32 [64, 256], replicated
All inputs are finite; a program needn't handle non-finite values.
Results may differ from a plain program's by a relative error of at most 0.035.
Values may be sent and summed in bfloat16 or wider, within the bound.
No kernel may reach another device: no remote copies, remote signals or barrier semaphores. Data moves between devices by JAX's collectives and lax.ppermute only.
A program may use at most 192 MiB of HBM per device.

v0:
```python
import math
import jax
import jax.numpy as jnp
from jax import lax
from jax.sharding import PartitionSpec as P

HEADS = 14
KVH = 2
HD = 128
rope_base = 1000000.0
norm_eps = 1e-06


def angle_tables(first_pos, length):
    position = (first_pos + jnp.arange(length, dtype=jnp.int32)).astype(jnp.float32)
    frequency = rope_base ** (-(2.0 * jnp.arange(HD // 2, dtype=jnp.float32)) / HD)
    angles = position[:, None] * frequency[None, :]
    return (jnp.cos(angles), jnp.sin(angles))


def rotate(tensor, cosine, sine_table, signed):
    layout = (cosine.shape[0],) + (1,) * (tensor.ndim - 2) + (cosine.shape[1],)
    cosine = cosine.reshape(layout)
    sine_part = sine_table.reshape(layout) * signed
    half_width = tensor.shape[-1] // 2
    first_half = tensor[..., :half_width]
    second_half = tensor[..., half_width:]
    return jnp.concatenate(
        [
            first_half * cosine - second_half * sine_part,
            second_half * cosine + first_half * sine_part,
        ],
        axis=-1,
    )


def on_device(
    thinker_normed,
    thinker_resid,
    gate_weight,
    up_weight,
    down_weight,
    bridge_weight,
    talker_stream,
    norm_gain,
    w_query,
    w_key,
    w_value,
    a_query,
    b_query,
    a_value,
    b_value,
    text_index,
    span_offset,
    out_grad,
):
    seq_count, rows_seq, columns = thinker_normed.shape
    normed = thinker_normed.reshape(seq_count * rows_seq, columns)
    ff_local = gate_weight.shape[1]
    block = normed
    gate_part = jnp.dot(block, gate_weight, preferred_element_type=jnp.float32)
    up_part = jnp.dot(block, up_weight, preferred_element_type=jnp.float32)
    both_parts = lax.psum_scatter(
        jnp.concatenate([gate_part, up_part], axis=1), "gx", scatter_dimension=0, tiled=True
    )
    hidden = (jax.nn.silu(both_parts[:, :ff_local]) * both_parts[:, ff_local:]).astype(jnp.bfloat16)
    partial_out = jnp.dot(
        lax.all_gather(hidden, "gx", axis=0, tiled=True),
        down_weight,
        preferred_element_type=jnp.float32,
    )
    summed = lax.psum_scatter(partial_out, "gy", scatter_dimension=0, tiled=True)
    thinker_out = (summed + thinker_resid[0].astype(jnp.float32)).astype(jnp.bfloat16)
    bridge_part = jnp.dot(thinker_out, bridge_weight, preferred_element_type=jnp.float32)
    bridge = lax.psum(bridge_part, "gx").astype(jnp.bfloat16)
    tokens = talker_stream.shape[1]
    groups = HEADS // KVH
    scale = 1.0 / math.sqrt(HD)
    picks = (text_index[0][:, None] == jnp.arange(rows_seq, dtype=jnp.int32)[None, :]).astype(
        jnp.bfloat16
    )
    mixed = talker_stream[0].astype(jnp.float32) + jnp.dot(
        picks, bridge, preferred_element_type=jnp.float32
    )
    normal = (
        mixed * lax.rsqrt(jnp.mean(mixed * mixed, axis=1, keepdims=True) + norm_eps) * norm_gain
    ).astype(jnp.bfloat16)
    low_query = jnp.dot(normal, a_query, preferred_element_type=jnp.float32).astype(jnp.bfloat16)
    low_value = jnp.dot(normal, a_value, preferred_element_type=jnp.float32).astype(jnp.bfloat16)
    slab_rows = lax.all_gather(normal, "gy", axis=0, tiled=True)
    projected = jnp.concatenate(
        [
            jnp.dot(slab_rows, w_query, preferred_element_type=jnp.float32),
            jnp.dot(slab_rows, w_key, preferred_element_type=jnp.float32),
            jnp.dot(slab_rows, w_value, preferred_element_type=jnp.float32),
        ],
        axis=1,
    )
    returned = lax.all_to_all(projected, "gy", split_axis=0, concat_axis=1, tiled=True)
    parcels = returned.reshape(tokens, lax.axis_size("gy"), -1)
    query_cols = w_query.shape[1]
    key_cols = w_key.shape[1]
    base_query = parcels[:, :, :query_cols].reshape(tokens, -1)
    base_key = parcels[:, :, query_cols : query_cols + key_cols].reshape(tokens, -1)
    base_value = parcels[:, :, query_cols + key_cols :].reshape(tokens, -1)
    first_pos = lax.axis_index("gx") * tokens
    cosine, sine_table = angle_tables(first_pos, tokens)
    query_pre = base_query + jnp.dot(low_query, b_query, preferred_element_type=jnp.float32)
    query = rotate(query_pre.reshape(tokens, KVH, groups, HD), cosine, sine_table, 1.0).astype(
        jnp.bfloat16
    )
    key_local = (
        rotate(base_key.reshape(tokens, KVH, HD), cosine, sine_table, 1.0)
        .astype(jnp.bfloat16)
        .reshape(tokens, KVH * HD)
    )
    value_local = (
        base_value + jnp.dot(low_value, b_value, preferred_element_type=jnp.float32)
    ).astype(jnp.bfloat16)
    key_all, value_all = (
        lax.all_gather(key_local, "gx", axis=0, tiled=True),
        lax.all_gather(value_local, "gx", axis=0, tiled=True),
    )
    length = key_all.shape[0]
    key_rows = key_all.reshape(length, KVH, HD)
    value_rows = value_all.reshape(length, KVH, HD)
    query_places = first_pos + jnp.arange(tokens, dtype=jnp.int32)
    key_places = jnp.arange(length, dtype=jnp.int32)
    causal = (key_places[None, :] <= query_places[:, None]) | (key_places[None, :] < span_offset[0])
    scores = (
        jnp.einsum("tkgd,skd->kgts", query, key_rows, preferred_element_type=jnp.float32) * scale
    )
    scores = jnp.where(causal, scores, -1e30)
    row_max = jnp.max(scores, axis=-1, keepdims=True)
    weights = jnp.exp(scores - row_max)
    probs = (weights / jnp.sum(weights, axis=-1, keepdims=True)).astype(jnp.bfloat16)
    attended = jnp.einsum(
        "kgts,skd->tkgd", probs, value_rows, preferred_element_type=jnp.float32
    ).astype(jnp.bfloat16)
    grad_four = out_grad[0].reshape(tokens, KVH, groups, HD)
    inner_prod = jnp.sum(grad_four.astype(jnp.float32) * attended.astype(jnp.float32), axis=-1)
    dprob = jnp.einsum("tkgd,skd->kgts", grad_four, value_rows, preferred_element_type=jnp.float32)
    dscore = (
        probs.astype(jnp.float32) * (dprob - jnp.transpose(inner_prod, (1, 2, 0))[..., None])
    ).astype(jnp.bfloat16)
    dquery = (
        jnp.einsum("kgts,skd->tkgd", dscore, key_rows, preferred_element_type=jnp.float32) * scale
    )
    query_grad = (
        rotate(dquery, cosine, sine_table, -1.0).reshape(tokens, HEADS * HD).astype(jnp.bfloat16)
    )
    block = probs
    term = jnp.einsum("kgts,tkgd->skd", block, grad_four, preferred_element_type=jnp.float32)
    value_grad = lax.psum_scatter(
        term.reshape(lax.axis_size("gx") * tokens, KVH * HD), "gx", scatter_dimension=0, tiled=True
    ).astype(jnp.bfloat16)
    part_bq = jnp.einsum("tr,tc->rc", low_query, query_grad, preferred_element_type=jnp.float32)
    part_bv = jnp.einsum("tr,tc->rc", low_value, value_grad, preferred_element_type=jnp.float32)
    dlow_query = jnp.einsum(
        "tc,rc->tr", query_grad, b_query, preferred_element_type=jnp.float32
    ).astype(jnp.bfloat16)
    dlow_value = jnp.einsum(
        "tc,rc->tr", value_grad, b_value, preferred_element_type=jnp.float32
    ).astype(jnp.bfloat16)
    part_aq = jnp.einsum("td,tr->dr", normal, dlow_query, preferred_element_type=jnp.float32)
    part_av = jnp.einsum("td,tr->dr", normal, dlow_value, preferred_element_type=jnp.float32)
    grad_aq, grad_bq, grad_av, grad_bv = lax.psum(
        (part_aq, part_bq, part_av, part_bv), ("gx", "gy")
    )
    attn_out = attended.reshape(1, tokens, HEADS * HD)
    return (attn_out, grad_aq, grad_bq, grad_av, grad_bv)


def solution(mesh):
    return jax.shard_map(
        on_device,
        mesh=mesh,
        in_specs=(
            P(None, None, "gx"),
            P("gy", None, "gx"),
            P("gx", "gy"),
            P("gx", "gy"),
            P("gy", "gx"),
            P("gx", None),
            P("gy", "gx", None),
            P(),
            P(None, "gy"),
            P(None, "gy"),
            P(None, "gy"),
            P(),
            P(),
            P(),
            P(),
            P("gy", "gx"),
            P("gy"),
            P("gy", "gx", None),
        ),
        out_specs=(P("gy", "gx", None), P(), P(), P(), P()),
        check_vma=False,
    )
```

profile of v0, /device:TPU:0, one launch (start us, length us, event | category | flops | bytes accessed | tf_op | source)
XLA Modules:
  0.0 564.3 jit_solution(9775176805287978987)
XLA Ops:
  7.2 10.2 %fusion.54 = f32[64,7392]{1,0:T(8,128)S(1)} fusion(bf16[64,1024]{1,0:T(8,128)(2,1)} %bitcast.100, bf16[1024,7392]{0,1:T(8,128)(2,1)} %param.20), kind=kOutput, calls=%fused_computation.78 | convolution fusion | flops 968884224 | bytes 17162240 | tf_op jit(solution)/shard_map/dot_general | solution.py:61
  17.4 10.0 %fusion.55 = f32[64,7392]{1,0:T(8,128)S(1)} fusion(bf16[64,1024]{1,0:T(8,128)(2,1)S(1)} %bitcast.101, bf16[1024,7392]{0,1:T(8,128)(2,1)} %param.21), kind=kOutput, calls=%fused_computation.79 | convolution fusion | flops 968884224 | bytes 17162240 | tf_op jit(solution)/shard_map/dot_general | solution.py:62
  27.4 2.5 pad_maximum_fusion
  29.9 52.0 %reduce-scatter.6.cloned.1.call-done = f32[8,14784]{1,0:T(8,128)} async-done(((f32[64,14784]{1,0:T(8,128)}), f32[8,14784]{1,0:T(8,128)}) %reduce-scatter.6.cloned.1.call-update) | async-done | bytes 473104 | tf_op jit(solution)/shard_map/reduce_scatter | solution.py:63
  81.9 1.2 fusion.32
  83.1 10.8 %all_gather.12 = bf16[64,7392]{1,0:T(8,128)(2,1)S(1)} all-gather(bf16[8,7392]{1,0:T(8,128)(2,1)S(1)} %fusion.32), channel_id=1, replica_groups=mesh['gx'=8,'gy'=4] {'gx'}, dimensions={0}, use_global_device_ids=true | all-gather | bytes 1064448 | tf_op jit(solution)/shard_map/all_gather | solution.py:68
  93.9 8.8 %fusion.56 = f32[64,1024]{1,0:T(8,128)} fusion(bf16[64,7392]{1,0:T(8,128)(2,1)S(1)} %all_gather.12, bf16[7392,1024]{1,0:T(8,128)(2,1)} %param.22), kind=kOutput, calls=%fused_computation.80 | convolution fusion | flops 968884224 | bytes 16347136 | tf_op jit(solution)/shard_map/dot_general | solution.py:67
  102.7 20.1 %reduce-scatter.8.cloned.1.call-done = f32[16,1024]{1,0:T(8,128)} async-done(((f32[64,1024]{1,0:T(8,128)}), f32[16,1024]{1,0:T(8,128)}) %reduce-scatter.8.cloned.1.call-update) | async-done | bytes 65552 | tf_op jit(solution)/shard_map/reduce_scatter | solution.py:72
  122.8 4.2 fusion.41
  127.0 25.4 %all-reduce.5 = bf16[16,3584]{1,0:T(8,128)(2,1)S(1)} all-reduce(f32[16,3584]{1,0:T(8,128)S(1)} %fusion.41), channel_id=1, replica_groups=mesh['gx'=8,'gy'=4] {'gx'}, use_global_device_ids=true, to_apply=%region_2.3 | all-reduce | flops 57344 | bytes 344064 | tf_op jit(solution)/shard_map/psum | solution.py:75
  152.4 2.0 multiply_reduce_fusion
  154.4 1.5 multiply_convert_fusion
  155.9 99.9 %all-gather.2.cloned.1.call-done = bf16[768,3584]{1,0:T(8,128)(2,1)} async-done(((bf16[192,3584]{1,0:T(8,128)(2,1)}), bf16[768,3584]{1,0:T(8,128)(2,1)}) %all-gather.2.cloned.1.call-update) | async-done | bytes 5505040 | tf_op jit(solution)/shard_map/all_gather | solution.py:90
  255.8 5.4 fusion.57
  261.2 1.8 fusion.58
  263.0 1.8 fusion.59
  264.9 1.8 copy.44
  266.7 4.6 all-to-all-start
  273.9 1.7 reshape_squeeze.3
  277.1 1.6 convolution_convert_fusion.4
  278.7 38.4 %all-to-all-done = f32[4,192,576]{2,1,0:T(8,128)} async-done(((f32[4,192,576]{2,1,0:T(8,128)}), f32[4,192,576]{2,1,0:T(8,128)}, u32[]{:S(2)}, u32[]{:S(2)}) %all-to-all-start) | async-done | bytes 1769504 | tf_op jit(solution)/shard_map/all_to_all | solution.py:99
  317.0 1.5 slice.50
  318.6 2.1 fusion.51
  320.7 2.2 copy.52
  322.8 2.5 reshape.208
  325.3 1.5 convolution_add_fusion.1
  326.8 1.7 reshape.209
  328.4 2.1 fusion.52
  330.6 1.2 copy.47
  332.9 11.6 %all_gather.15 = bf16[1536,256]{1,0:T(8,128)(2,1)} all-gather(bf16[192,256]{1,0:T(8,128)(2,1)S(1)} %copy.50), channel_id=1, replica_groups=mesh['gx'=8,'gy'=4] {'gx'}, dimensions={0}, use_global_device_ids=true | all-gather | bytes 884736 | tf_op jit(solution)/shard_map/all_gather | solution.py:121
  344.5 2.3 copy.51
  346.8 3.4 subtract_convert_fusion.1
  350.2 10.5 %fusion.53 = (f32[2,7,192]{2,1,0:T(8,128)S(1)}, f32[2,7,192,1536]{3,2,1,0:T(8,128)}) fusion(pred[192,1536]{1,0:T(8,128)(4,1)S(1)} %copy-done.19, bf16[1536,2,128,1]{0,2,3,1:T(8,128)(2,1)} %bitcast.104, bf16[192,2,7,64]{3,0,2,1:T(8,128)(2,1)} %get-tuple-element.10, bf16[192,2,7,64]{3,0,2,1:T(8,128)(2,1)} %get-tuple-element.9), kind=kOutput, calls=%fused_computation.77 | convolution fusion | flops 1074857472 | bytes 18295296 | tf_op jit(solution)/shard_map/sub | solution.py:135
  360.8 7.1 %divide_convert_fusion = bf16[2,7,192,1536]{3,2,1,0:T(8,128)(2,1)S(1)} fusion(f32[2,7,192,1536]{3,2,1,0:T(8,128)} %get-tuple-element.25, f32[2,7,192]{2,1,0:T(8,128)S(1)} %get-tuple-element.24), kind=kLoop, calls=%fused_computation.5 | loop fusion | flops 8257536 | bytes 24783360 | tf_op jit(solution)/shard_map/convert_element_type | solution.py:136
  367.9 1.5 fusion.28
  369.4 1.7 copy-done.2
  371.1 1.7 copy.77
  372.8 1.2 copy.45
  374.4 11.2 %all_gather.14 = bf16[1536,256]{1,0:T(8,128)(2,1)} all-gather(bf16[192,256]{1,0:T(8,128)(2,1)S(1)} %fusion.22), channel_id=1, replica_groups=mesh['gx'=8,'gy'=4] {'gx'}, dimensions={0}, use_global_device_ids=true | all-gather | bytes 884736 | tf_op jit(solution)/shard_map/all_gather | solution.py:122
  385.7 2.2 reshape.206
  387.9 6.6 %multiply_reduce_fusion.1 = (f32[192,2,7]{0,2,1:T(8,128)S(1)}, bf16[192,2,7,128]{3,0,2,1:T(8,128)(2,1)}) fusion(bf16[192,2,7,128]{3,2,1,0:T(8,128)(2,1)S(1)} %copy-done.7, bf16[2,7,192,1536]{3,2,1,0:T(8,128)(2,1)} %copy-done.2, bf16[1536,2,128,1]{2,1,0,3:T(2,128)(2,1)S(1)} %bitcast.98), kind=kOutput, calls=%fused_computation.25 | convolution fusion | flops 1058682240 | bytes 10430976 | tf_op jit(solution)/shard_map/kgts,skd->tkgd/dot_general | solution.py:137
  394.6 9.5 %fusion.17 = f32[192,2,7,128]{3,0,2,1:T(8,128)} fusion(bf16[1536,2,128,1]{0,2,3,1:T(8,128)(2,1)} %bitcast.105, bf16[2,7,192,1536]{3,2,1,0:T(8,128)(2,1)} %copy-done.2, f32[2,7,192]{2,1,0:T(8,128)S(1)} %bitcast.107, bf16[1536,2,128,1]{2,1,0,3:T(2,128)(2,1)S(1)} %bitcast.99, bf16[192,2,7,128]{3,2,1,0:T(8,128)(2,1)S(1)} %copy-done.7), kind=kOutput, calls=%fused_computation.22 | convolution fusion | flops 2130788352 | bytes 11905536 | tf_op jit(solution)/shard_map/kgts,skd->tkgd/dot_general | solution.py:147
  404.0 2.3 subtract_convert_fusion
  409.0 1.9 fusion.23
  412.8 1.4 fusion.24
  414.7 1.6 reshape.210
  416.3 136.6 %all-reduce.4.cloned.1.call-done = (f32[3584,64]{0,1:T(8,128)}, f32[64,1792]{1,0:T(8,128)}, f32[3584,64]{0,1:T(8,128)}, f32[64,256]{1,0:T(8,128)}) async-done(((f32[3584,64]{0,1:T(8,128)}, f32[64,1792]{1,0:T(8,128)}, f32[3584,64]{0,1:T(8,128)}, f32[64,256]{1,0:T(8,128)}), (f32[3584,64]{0,1:T(8,128)}, f32[64,1792]{1,0:T(8,128)}, f32[3584,64]{0,1:T(8,128)}, f32[64,256]{1,0:T(8,128)})) %all-reduce.4.cloned.1.call-update) | async-done | bytes 2359312 | tf_op jit(solution)/shard_map/psum | solution.py:167
  552.9 2.3 copy.105
  (84 shorter events, 12.6 us)
Async XLA Ops:
  7.2 248.6 %copy-start = (bf16[3584,448]{0,1:T(8,128)(2,1)S(1)}, bf16[3584,448]{0,1:T(8,128)(2,1)}, u32[]{:S(2)}) copy-start(bf16[3584,448]{0,1:T(8,128)(2,1)} %param.26) | copy-start | bytes 9633796
  7.2 74.7 %reduce-scatter.6.cloned.1.call-start = ((), (), s32[]{:S(2)}) async-start(), calls=%async_computation.4 | async-start | bytes 4276224 | tf_op jit(solution)/shard_map/reduce_scatter | solution.py:63
  7.2 10.2 %copy-start.9 = (bf16[4,16,1024]{2,1,0:T(8,128)(2,1)S(1)}, bf16[4,16,1024]{2,1,0:T(8,128)(2,1)}, u32[]{:S(2)}) copy-start(bf16[4,16,1024]{2,1,0:T(8,128)(2,1)} %param.18) | copy-start | bytes 393220
  29.9 92.9 %reduce-scatter.8.cloned.1.call-start = ((), (), s32[]{:S(2)}) async-start(), calls=%async_computation.5 | async-start | bytes 327680 | tf_op jit(solution)/shard_map/reduce_scatter | solution.py:72
  93.9 29.0 %copy-start.22 = (bf16[1,16,1024]{2,1,0:T(8,128)(2,1)S(1)}, bf16[1,16,1024]{2,1,0:T(8,128)(2,1)}, u32[]{:S(2)}) copy-start(bf16[1,16,1024]{2,1,0:T(8,128)(2,1)} %param.19) | copy-start | bytes 98308
  102.7 153.1 %all-gather.2.cloned.1.call-start = ((), (), s32[]{:S(2)}) async-start(), calls=%async_computation.6 | async-start | bytes 6881280 | tf_op jit(solution)/shard_map/all_gather | solution.py:90
  152.4 2.0 copy-start.23
  255.8 5.4 copy-start.4
  255.8 5.4 copy-start.14
  261.2 1.8 copy-start.15
  266.7 7.2 %copy-start.13 = (bf16[1,192,1792]{2,1,0:T(8,128)(2,1)S(1)}, bf16[1,192,1792]{2,1,0:T(8,128)(2,1)}, u32[]{:S(2)}) copy-start(bf16[1,192,1792]{2,1,0:T(8,128)(2,1)} %param.35) | copy-start | bytes 2064388
  266.7 50.3 %all-to-all-start = ((f32[4,192,576]{2,1,0:T(8,128)}), f32[4,192,576]{2,1,0:T(8,128)}, u32[]{:S(2)}, u32[]{:S(2)}) async-start(f32[4,192,576]{2,1,0:T(8,128)} %bitcast.4), calls=%async_computation.2 | async-start | bytes 3932160 | tf_op jit(solution)/shard_map/all_to_all | solution.py:99
  271.2 5.3 copy-start.3
  271.3 5.3 copy-start.16
  271.3 139.6 %reduce-scatter.10.cloned.1.call-start = ((), (), s32[]{:S(2)}) async-start(), calls=%async_computation.7 | async-start | bytes 1769472
  322.8 2.5 copy-start.10
  331.8 15.0 %copy-start.5 = (f32[192,2,7,64]{3,2,1,0:T(8,128)S(1)}, f32[192,2,7,64]{3,2,1,0:T(8,128)}, u32[]{:S(2)}) copy-start(f32[192,2,7,64]{3,2,1,0:T(8,128)} %get-tuple-element.15) | copy-start | bytes 2064388
  346.8 3.4 copy-start.19
  360.8 7.1 %copy-start.6 = (bf16[192,2,7,128]{3,2,1,0:T(8,128)(2,1)S(1)}, bf16[192,2,7,128]{3,2,1,0:T(8,128)(2,1)}, u32[]{:S(2)}) copy-start(bf16[192,2,7,128]{3,2,1,0:T(8,128)(2,1)} %reshape_squeeze.3) | copy-start | bytes 2064388
  367.9 3.2 copy-start.2
  372.7 1.5 copy-start.20
  372.8 180.1 %all-reduce.4.cloned.1.call-start = ((), (), s32[]{:S(2)}) async-start(), calls=%async_computation.8 | async-start | bytes 4718592 | tf_op jit(solution)/shard_map/psum | solution.py:167
  372.8 15.1 %copy-start.7 = (bf16[192,2,7,128]{3,2,1,0:T(8,128)(2,1)S(1)}, bf16[192,2,7,128]{3,2,1,0:T(8,128)(2,1)}, u32[]{:S(2)}) copy-start(bf16[192,2,7,128]{3,2,1,0:T(8,128)(2,1)} %reshape_squeeze.3) | copy-start | bytes 2064388
  394.6 9.5 %copy-start.18 = (f32[192,64]{1,0:T(8,128)S(1)}, f32[192,64]{1,0:T(8,128)}, u32[]{:S(2)}) copy-start(f32[192,64]{1,0:T(8,128)} %get-tuple-element.19) | copy-start | bytes 147460
  406.8 2.3 copy-start.11
  412.8 1.5 copy-start.8
  552.9 2.3 copy-start.17
  552.9 3.1 copy-start.12
  552.9 4.0 copy-start.21
  552.9 4.7 copy-start.1
Sparse Core Ops, SparseCore 0:
  30.0 51.8 reduce-scatter.5
  102.8 19.9 reduce-scatter.7
  156.0 99.6 all-gather.1
  372.9 36.5 reduce-scatter.9
  415.9 136.9 all-reduce.3
where the time goes:
time: 573 us; the launch traced here: 564 us
  waiting for transfers between devices  347 us (61%)
  matrix products  81.1 us (14%)
  blocking collectives  59 us (10%)
  local copies, waits for them, and re-layouts  35.9 us (6%)
  other arithmetic  21.5 us (4%)
  between operations  15.1 us (3%)
    psum x1, waiting for transfers between devices, on_device(): lax.psum((part_aq, part_bq, part_av, part_bv), ('gx', 'gy'))  137 us
    all_gather x1, waiting for transfers between devices, on_device(): slab_rows = lax.all_gather(normal, 'gy', axis=0, tiled=True)  99.9 us
    reduce_scatter x1, waiting for transfers between devices, on_device(): lax.psum_scatter(jnp.concatenate([gate_part, up_part], axis=1), 'gx', sca...  52 us
    all_to_all x1, waiting for transfers between devices, on_device(): lax.all_to_all(projected, 'gy', split_axis=0, concat_axis=1, tiled=True)  38.4 us
    psum x1, blocking collectives, on_device(): bridge = lax.psum(bridge_part, 'gx').astype(jnp.bfloat16)  25.4 us
    reduce_scatter x1, waiting for transfers between devices, on_device(): lax.psum_scatter(partial_out, 'gy', scatter_dimension=0, tiled=True)  20.1 us
    all_gather x1, blocking collectives, on_device(): lax.all_gather(key_local, 'gx', axis=0, tiled=True)  11.6 us
  transfers between devices with their start and end apart: 6, of which 5 were waited for; matrix products, arithmetic and copies ran while one was open for 6% of the time, Pallas kernels for 0%

commit v1 on v0

--- a/solution.py
+++ b/solution.py
@@ -1,14 +1,25 @@
+import functools
 import math
 import jax
 import jax.numpy as jnp
 from jax import lax
 from jax.sharding import PartitionSpec as P
+from jax.lax import psum
 
 HEADS = 14
 KVH = 2
 HD = 128
 rope_base = 1000000.0
 norm_eps = 1e-06
+
+
+def write_arrays_by_axis(u_in, link_axis, ax_name):
+    for nth in (link_axis, ax_name):
+        u_in = psum(u_in, nth)
+    return u_in
+
+
+_produce_turns = functools.partial(write_arrays_by_axis, link_axis="gx", ax_name="gy")
 
 
 def angle_tables(first_pos, length):
@@ -164,9 +175,7 @@
     ).astype(jnp.bfloat16)
     part_aq = jnp.einsum("td,tr->dr", normal, dlow_query, preferred_element_type=jnp.float32)
     part_av = jnp.einsum("td,tr->dr", normal, dlow_value, preferred_element_type=jnp.float32)
-    grad_aq, grad_bq, grad_av, grad_bv = lax.psum(
-        (part_aq, part_bq, part_av, part_bv), ("gx", "gy")
-    )
+    grad_aq, grad_bq, grad_av, grad_bv = _produce_turns((part_aq, part_bq, part_av, part_bv))
     attn_out = attended.reshape(1, tokens, HEADS * HD)
     return (attn_out, grad_aq, grad_bq, grad_av, grad_bv)
 

time: 573 us -> 594 us (1.037)
  waiting for transfers between devices: 347 us -> 367 us
    psum x1 -> x2, waiting for transfers between devices: 137 us -> 157 us  [write_arrays_by_axis(): u_in = psum(u_in, nth)]
  transfers between devices with their start and end apart: 6 -> 7, of which waited for: 5 -> 6; matrix products, arithmetic and copies ran while one was open for 6% -> 6% of each run, Pallas kernels for 0% -> 0%
where the time goes in v1:
time: 594 us; the launch traced here: 585 us
  waiting for transfers between devices  367 us (62%)
  matrix products  81.1 us (14%)
  blocking collectives  59.2 us (10%)
  local copies, waits for them, and re-layouts  35.7 us (6%)
  other arithmetic  21.5 us (4%)
  between operations  15.4 us (3%)
    psum x2, waiting for transfers between devices, write_arrays_by_axis(): u_in = psum(u_in, nth)  157 us
    all_gather x1, waiting for transfers between devices, on_device(): slab_rows = lax.all_gather(normal, 'gy', axis=0, tiled=True)  99.9 us
    reduce_scatter x1, waiting for transfers between devices, on_device(): lax.psum_scatter(jnp.concatenate([gate_part, up_part], axis=1), 'gx', sca...  52 us
    all_to_all x1, waiting for transfers between devices, on_device(): lax.all_to_all(projected, 'gy', split_axis=0, concat_axis=1, tiled=True)  38.4 us
    psum x1, blocking collectives, on_device(): bridge = lax.psum(bridge_part, 'gx').astype(jnp.bfloat16)  25.4 us
    reduce_scatter x1, waiting for transfers between devices, on_device(): lax.psum_scatter(partial_out, 'gy', scatter_dimension=0, tiled=True)  20.1 us
  transfers between devices with their start and end apart: 7, of which 6 were waited for; matrix products, arithmetic and copies ran while one was open for 6% of the time, Pallas kernels for 0%

profile of v1, /device:TPU:0, one launch (start us, length us, event | category | flops | bytes accessed | tf_op | source)
XLA Modules:
  0.0 585.2 jit_solution(6508595556607797959)
XLA Ops:
  7.2 10.2 %fusion.54 = f32[64,7392]{1,0:T(8,128)S(1)} fusion(bf16[64,1024]{1,0:T(8,128)(2,1)} %bitcast.100, bf16[1024,7392]{0,1:T(8,128)(2,1)} %param.20), kind=kOutput, calls=%fused_computation.78 | convolution fusion | flops 968884224 | bytes 17162240 | tf_op jit(solution)/shard_map/dot_general | solution.py:72
  17.4 10.0 %fusion.55 = f32[64,7392]{1,0:T(8,128)S(1)} fusion(bf16[64,1024]{1,0:T(8,128)(2,1)S(1)} %bitcast.101, bf16[1024,7392]{0,1:T(8,128)(2,1)} %param.21), kind=kOutput, calls=%fused_computation.79 | convolution fusion | flops 968884224 | bytes 17162240 | tf_op jit(solution)/shard_map/dot_general | solution.py:73
  27.4 2.5 pad_maximum_fusion
  30.0 52.0 %reduce-scatter.6.cloned.1.call-done = f32[8,14784]{1,0:T(8,128)} async-done(((f32[64,14784]{1,0:T(8,128)}), f32[8,14784]{1,0:T(8,128)}) %reduce-scatter.6.cloned.1.call-update) | async-done | bytes 473104 | tf_op jit(solution)/shard_map/reduce_scatter | solution.py:74
  81.9 1.2 fusion.32
  83.1 10.8 %all_gather.12 = bf16[64,7392]{1,0:T(8,128)(2,1)S(1)} all-gather(bf16[8,7392]{1,0:T(8,128)(2,1)S(1)} %fusion.32), channel_id=1, replica_groups=mesh['gx'=8,'gy'=4] {'gx'}, dimensions={0}, use_global_device_ids=true | all-gather | bytes 1064448 | tf_op jit(solution)/shard_map/all_gather | solution.py:79
  93.9 8.8 %fusion.56 = f32[64,1024]{1,0:T(8,128)} fusion(bf16[64,7392]{1,0:T(8,128)(2,1)S(1)} %all_gather.12, bf16[7392,1024]{1,0:T(8,128)(2,1)} %param.22), kind=kOutput, calls=%fused_computation.80 | convolution fusion | flops 968884224 | bytes 16347136 | tf_op jit(solution)/shard_map/dot_general | solution.py:78
  102.8 20.1 %reduce-scatter.8.cloned.1.call-done = f32[16,1024]{1,0:T(8,128)} async-done(((f32[64,1024]{1,0:T(8,128)}), f32[16,1024]{1,0:T(8,128)}) %reduce-scatter.8.cloned.1.call-update) | async-done | bytes 65552 | tf_op jit(solution)/shard_map/reduce_scatter | solution.py:83
  122.8 4.2 fusion.41
  127.0 25.4 %all-reduce.9 = bf16[16,3584]{1,0:T(8,128)(2,1)S(1)} all-reduce(f32[16,3584]{1,0:T(8,128)S(1)} %fusion.41), channel_id=1, replica_groups=mesh['gx'=8,'gy'=4] {'gx'}, use_global_device_ids=true, to_apply=%region_2.3 | all-reduce | flops 57344 | bytes 344064 | tf_op jit(solution)/shard_map/psum | solution.py:86
  152.4 2.0 multiply_reduce_fusion
  154.5 1.5 multiply_convert_fusion
  155.9 99.9 %all-gather.2.cloned.1.call-done = bf16[768,3584]{1,0:T(8,128)(2,1)} async-done(((bf16[192,3584]{1,0:T(8,128)(2,1)}), bf16[768,3584]{1,0:T(8,128)(2,1)}) %all-gather.2.cloned.1.call-update) | async-done | bytes 5505040 | tf_op jit(solution)/shard_map/all_gather | solution.py:101
  255.8 5.4 fusion.57
  261.2 1.8 fusion.58
  263.0 1.8 fusion.59
  264.9 1.8 copy.44
  266.7 4.6 all-to-all-start
  273.9 1.7 reshape_squeeze.3
  277.1 1.6 convolution_convert_fusion.4
  278.7 38.4 %all-to-all-done = f32[4,192,576]{2,1,0:T(8,128)} async-done(((f32[4,192,576]{2,1,0:T(8,128)}), f32[4,192,576]{2,1,0:T(8,128)}, u32[]{:S(2)}, u32[]{:S(2)}) %all-to-all-start) | async-done | bytes 1769504 | tf_op jit(solution)/shard_map/all_to_all | solution.py:110
  317.0 1.5 slice.50
  318.6 2.1 fusion.51
  320.7 2.2 copy.52
  322.9 2.5 reshape.208
  325.3 1.5 convolution_add_fusion.1
  326.8 1.7 reshape.209
  328.5 2.2 fusion.52
  333.0 11.6 %all_gather.15 = bf16[1536,256]{1,0:T(8,128)(2,1)} all-gather(bf16[192,256]{1,0:T(8,128)(2,1)S(1)} %copy.50), channel_id=1, replica_groups=mesh['gx'=8,'gy'=4] {'gx'}, dimensions={0}, use_global_device_ids=true | all-gather | bytes 884736 | tf_op jit(solution)/shard_map/all_gather | solution.py:132
  344.6 2.3 copy.51
  346.9 3.4 subtract_convert_fusion.1
  350.3 10.6 %fusion.53 = (f32[2,7,192]{2,1,0:T(8,128)S(1)}, f32[2,7,192,1536]{3,2,1,0:T(8,128)}) fusion(pred[192,1536]{1,0:T(8,128)(4,1)S(1)} %copy-done.19, bf16[1536,2,128,1]{0,2,3,1:T(8,128)(2,1)} %bitcast.104, bf16[192,2,7,64]{3,0,2,1:T(8,128)(2,1)} %get-tuple-element.14, bf16[192,2,7,64]{3,0,2,1:T(8,128)(2,1)} %get-tuple-element.13), kind=kOutput, calls=%fused_computation.77 | convolution fusion | flops 1074857472 | bytes 18295296 | tf_op jit(solution)/shard_map/sub | solution.py:146
  360.9 7.1 %divide_convert_fusion = bf16[2,7,192,1536]{3,2,1,0:T(8,128)(2,1)S(1)} fusion(f32[2,7,192,1536]{3,2,1,0:T(8,128)} %get-tuple-element.29, f32[2,7,192]{2,1,0:T(8,128)S(1)} %get-tuple-element.28), kind=kLoop, calls=%fused_computation.5 | loop fusion | flops 8257536 | bytes 24783360 | tf_op jit(solution)/shard_map/convert_element_type | solution.py:147
  367.9 1.5 fusion.28
  369.4 1.7 copy-done.2
  371.1 1.7 copy.77
  372.9 1.2 copy.45
  374.5 11.5 %all_gather.14 = bf16[1536,256]{1,0:T(8,128)(2,1)} all-gather(bf16[192,256]{1,0:T(8,128)(2,1)S(1)} %fusion.22), channel_id=1, replica_groups=mesh['gx'=8,'gy'=4] {'gx'}, dimensions={0}, use_global_device_ids=true | all-gather | bytes 884736 | tf_op jit(solution)/shard_map/all_gather | solution.py:133
  386.0 2.0 reshape.206
  388.0 6.6 %multiply_reduce_fusion.1 = (f32[192,2,7]{0,2,1:T(8,128)S(1)}, bf16[192,2,7,128]{3,0,2,1:T(8,128)(2,1)}) fusion(bf16[192,2,7,128]{3,2,1,0:T(8,128)(2,1)S(1)} %copy-done.7, bf16[2,7,192,1536]{3,2,1,0:T(8,128)(2,1)} %copy-done.2, bf16[1536,2,128,1]{2,1,0,3:T(2,128)(2,1)S(1)} %bitcast.98), kind=kOutput, calls=%fused_computation.25 | convolution fusion | flops 1058682240 | bytes 10430976 | tf_op jit(solution)/shard_map/kgts,skd->tkgd/dot_general | solution.py:148
  394.7 9.5 %fusion.17 = f32[192,2,7,128]{3,0,2,1:T(8,128)} fusion(bf16[1536,2,128,1]{0,2,3,1:T(8,128)(2,1)} %bitcast.105, bf16[2,7,192,1536]{3,2,1,0:T(8,128)(2,1)} %copy-done.2, f32[2,7,192]{2,1,0:T(8,128)S(1)} %bitcast.107, bf16[1536,2,128,1]{2,1,0,3:T(2,128)(2,1)S(1)} %bitcast.99, bf16[192,2,7,128]{3,2,1,0:T(8,128)(2,1)S(1)} %copy-done.7), kind=kOutput, calls=%fused_computation.22 | convolution fusion | flops 2130788352 | bytes 11905536 | tf_op jit(solution)/shard_map/kgts,skd->tkgd/dot_general | solution.py:158
  404.1 2.3 subtract_convert_fusion
  409.1 1.9 fusion.23
  412.9 1.4 fusion.24
  414.4 62.5 %all-reduce.6.cloned.1.call-done = (f32[3584,64]{0,1:T(8,128)}, f32[64,1792]{1,0:T(8,128)}, f32[3584,64]{0,1:T(8,128)}, f32[64,256]{1,0:T(8,128)}) async-done(((f32[3584,64]{0,1:T(8,128)}, f32[64,1792]{1,0:T(8,128)}, f32[3584,64]{0,1:T(8,128)}, f32[64,256]{1,0:T(8,128)}), (f32[3584,64]{0,1:T(8,128)}, f32[64,1792]{1,0:T(8,128)}, f32[3584,64]{0,1:T(8,128)}, f32[64,256]{1,0:T(8,128)})) %all-reduce.6.cloned.1.call-update) | async-done | bytes 2359312 | tf_op jit(solution)/shard_map/psum | solution.py:18
  477.4 1.6 reshape.210
  479.0 94.5 %all-reduce.8.cloned.1.call-done = (f32[3584,64]{0,1:T(8,128)}, f32[64,1792]{1,0:T(8,128)}, f32[3584,64]{0,1:T(8,128)}, f32[64,256]{1,0:T(8,128)}) async-done(((f32[3584,64]{0,1:T(8,128)}, f32[64,1792]{1,0:T(8,128)}, f32[3584,64]{0,1:T(8,128)}, f32[64,256]{1,0:T(8,128)}), (f32[3584,64]{0,1:T(8,128)}, f32[64,1792]{1,0:T(8,128)}, f32[3584,64]{0,1:T(8,128)}, f32[64,256]{1,0:T(8,128)})) %all-reduce.8.cloned.1.call-update) | async-done | bytes 2359312 | tf_op jit(solution)/shard_map/psum | solution.py:18
  573.5 2.3 copy.109
  (87 shorter events, 13.8 us)
Async XLA Ops:
  7.2 248.6 %copy-start = (bf16[3584,448]{0,1:T(8,128)(2,1)S(1)}, bf16[3584,448]{0,1:T(8,128)(2,1)}, u32[]{:S(2)}) copy-start(bf16[3584,448]{0,1:T(8,128)(2,1)} %param.26) | copy-start | bytes 9633796
  7.2 74.8 %reduce-scatter.6.cloned.1.call-start = ((), (), s32[]{:S(2)}) async-start(), calls=%async_computation.4 | async-start | bytes 4276224 | tf_op jit(solution)/shard_map/reduce_scatter | solution.py:74
  7.2 10.2 %copy-start.9 = (bf16[4,16,1024]{2,1,0:T(8,128)(2,1)S(1)}, bf16[4,16,1024]{2,1,0:T(8,128)(2,1)}, u32[]{:S(2)}) copy-start(bf16[4,16,1024]{2,1,0:T(8,128)(2,1)} %param.18) | copy-start | bytes 393220
  29.9 92.9 %reduce-scatter.8.cloned.1.call-start = ((), (), s32[]{:S(2)}) async-start(), calls=%async_computation.5 | async-start | bytes 327680 | tf_op jit(solution)/shard_map/reduce_scatter | solution.py:83
  93.9 29.0 %copy-start.22 = (bf16[1,16,1024]{2,1,0:T(8,128)(2,1)S(1)}, bf16[1,16,1024]{2,1,0:T(8,128)(2,1)}, u32[]{:S(2)}) copy-start(bf16[1,16,1024]{2,1,0:T(8,128)(2,1)} %param.19) | copy-start | bytes 98308
  102.7 153.1 %all-gather.2.cloned.1.call-start = ((), (), s32[]{:S(2)}) async-start(), calls=%async_computation.6 | async-start | bytes 6881280 | tf_op jit(solution)/shard_map/all_gather | solution.py:101
  152.4 2.0 copy-start.23
  255.8 5.4 copy-start.4
  255.8 5.4 copy-start.14
  261.2 1.8 copy-start.15
  266.7 7.2 %copy-start.13 = (bf16[1,192,1792]{2,1,0:T(8,128)(2,1)S(1)}, bf16[1,192,1792]{2,1,0:T(8,128)(2,1)}, u32[]{:S(2)}) copy-start(bf16[1,192,1792]{2,1,0:T(8,128)(2,1)} %param.35) | copy-start | bytes 2064388
  266.7 50.3 %all-to-all-start = ((f32[4,192,576]{2,1,0:T(8,128)}), f32[4,192,576]{2,1,0:T(8,128)}, u32[]{:S(2)}, u32[]{:S(2)}) async-start(f32[4,192,576]{2,1,0:T(8,128)} %bitcast.4), calls=%async_computation.2 | async-start | bytes 3932160 | tf_op jit(solution)/shard_map/all_to_all | solution.py:110
  271.3 5.3 copy-start.3
  271.3 5.3 copy-start.16
  271.3 139.7 %reduce-scatter.10.cloned.1.call-start = ((), (), s32[]{:S(2)}) async-start(), calls=%async_computation.7 | async-start | bytes 1769472
  322.9 2.5 copy-start.10
  331.8 15.0 %copy-start.5 = (f32[192,2,7,64]{3,2,1,0:T(8,128)S(1)}, f32[192,2,7,64]{3,2,1,0:T(8,128)}, u32[]{:S(2)}) copy-start(f32[192,2,7,64]{3,2,1,0:T(8,128)} %get-tuple-element.19) | copy-start | bytes 2064388
  346.9 3.4 copy-start.19
  360.9 7.1 %copy-start.6 = (bf16[192,2,7,128]{3,2,1,0:T(8,128)(2,1)S(1)}, bf16[192,2,7,128]{3,2,1,0:T(8,128)(2,1)}, u32[]{:S(2)}) copy-start(bf16[192,2,7,128]{3,2,1,0:T(8,128)(2,1)} %reshape_squeeze.3) | copy-start | bytes 2064388
  367.9 3.2 copy-start.2
  372.8 1.5 copy-start.20
  372.9 104.1 %all-reduce.6.cloned.1.call-start = ((), (), s32[]{:S(2)}) async-start(), calls=%async_computation.8 | async-start | bytes 4718592 | tf_op jit(solution)/shard_map/psum | solution.py:18
  372.9 15.1 %copy-start.7 = (bf16[192,2,7,128]{3,2,1,0:T(8,128)(2,1)S(1)}, bf16[192,2,7,128]{3,2,1,0:T(8,128)(2,1)}, u32[]{:S(2)}) copy-start(bf16[192,2,7,128]{3,2,1,0:T(8,128)(2,1)} %reshape_squeeze.3) | copy-start | bytes 2064388
  394.7 9.5 %copy-start.18 = (f32[192,64]{1,0:T(8,128)S(1)}, f32[192,64]{1,0:T(8,128)}, u32[]{:S(2)}) copy-start(f32[192,64]{1,0:T(8,128)} %get-tuple-element.23) | copy-start | bytes 147460
  406.9 2.3 copy-start.11
  414.3 62.6 %copy-start.8 = (bf16[192,2,7,128]{3,0,2,1:T(8,128)(2,1)S(1)}, bf16[192,2,7,128]{3,0,2,1:T(8,128)(2,1)}, u32[]{:S(2)}) copy-start(bf16[192,2,7,128]{3,0,2,1:T(8,128)(2,1)} %get-tuple-element.31) | copy-start | bytes 2064388
  414.3 159.2 %all-reduce.8.cloned.1.call-start = ((), (), s32[]{:S(2)}) async-start(), calls=%async_computation.9 | async-start | bytes 4718592 | tf_op jit(solution)/shard_map/psum | solution.py:18
  573.5 2.3 copy-start.17
  573.5 3.1 copy-start.12
  573.5 4.0 copy-start.21
  573.5 4.7 copy-start.1
Sparse Core Ops, SparseCore 0:
  30.0 51.8 reduce-scatter.5
  102.8 19.9 reduce-scatter.7
  156.1 99.6 all-gather.1
  373.0 36.4 reduce-scatter.9
  414.4 62.4 all-reduce.5
  479.4 94.0 all-reduce.7
